TPU v7x, 32 devices: a whole 2x2x4 slice. The times are simulated.
32 devices in a mesh: tm: 4 (over z), space: 8 (over y, x, core).
Axes of the slice: x: 2, y: 2, z: 4, core: 2. Of those that a mesh axis runs over, the one named last changes fastest.
Arguments:
- snapshots: bfloat16 [512, 393216], P('tm', 'space'), may hold values from -10 to 10, as said below
- area_weight: float32 [393216], P('space'), may hold values from 0.1 to 1
- eigvecs: bfloat16 [512, 64], replicated, may hold values from -0.25 to 0.25
- eigvals: float32 [64], replicated, may hold values from 0.5 to 8
Outputs:
- gram: float32 [512, 512], P(('tm', 'space'))
- modes: bfloat16 [64, 393216], P('tm', 'space')
Inputs may be any that keep to these rules, and one draw needn't show every extreme that they name: `snapshots`: a per-column climatology plus hourly departures.
All inputs are finite; a program needn't handle non-finite values.
Results may differ from a plain program's by a relative error of at most 0.01.
Values may be sent and summed in bfloat16 or wider, within the bound.
No kernel may reach another device: no remote copies, remote signals or barrier semaphores. Data moves between devices by JAX's collectives and lax.ppermute only.
A program may use at most 128 MiB of HBM per device.

v0:
```python
import jax
import jax.numpy as jnp
from jax import lax
from jax.sharding import PartitionSpec as P


def gram_local(weighted):
    return lax.dot_general(
        weighted, weighted, (((1,), (1,)), ((), ())), preferred_element_type=jnp.float32
    )


def local(snapshots, area_weight, eigvecs, eigvals):
    tm_count = lax.axis_size("tm")
    space_count = lax.axis_size("space")
    time_dev, cell_dev = snapshots.shape
    times = time_dev * tm_count
    cells = cell_dev * space_count
    sub_cells = cell_dev // tm_count
    tm_index = lax.axis_index("tm")
    columns = lax.all_to_all(snapshots, "tm", split_axis=1, concat_axis=0, tiled=True)
    mean = jnp.sum(columns.astype(jnp.float32), axis=0) / times
    root = jnp.sqrt(area_weight)
    own_root = lax.dynamic_slice_in_dim(root, tm_index * sub_cells, sub_cells, 0)
    weighted = (own_root[None, :] * (columns.astype(jnp.float32) - mean[None, :])).astype(
        jnp.bfloat16
    )
    partial_gram = gram_local(weighted) / cells
    row_sums = lax.psum_scatter(
        partial_gram.astype(jnp.bfloat16), "tm", scatter_dimension=0, tiled=True
    )
    gram = lax.psum_scatter(row_sums, "space", scatter_dimension=0, tiled=True).astype(jnp.float32)
    inv_root = 1.0 / jnp.sqrt(eigvals)
    projected = jnp.dot(eigvecs.T, weighted, preferred_element_type=jnp.float32)
    mode_piece = (projected * inv_root[:, None]).astype(jnp.bfloat16)
    modes = lax.all_to_all(mode_piece, "tm", split_axis=0, concat_axis=1, tiled=True)
    return (gram, modes)


def solution(mesh):
    in_specs = (P("tm", "space"), P("space"), P(), P())
    out_specs = (P(("tm", "space"), None), P("tm", "space"))
    return jax.shard_map(local, mesh=mesh, in_specs=in_specs, out_specs=out_specs, check_vma=False)
```

profile of v0, /device:TPU:0, one launch (start us, length us, event | category | flops | bytes accessed | tf_op | source)
XLA Modules:
  0.0 484.4 jit_solution(10182316372493514832)
XLA Ops:
  7.2 0.0 copy-start
  7.2 16.6 %copy.8 = bf16[128,49152]{0,1:T(8,128)(2,1)} copy(bf16[128,49152]{1,0:T(8,128)(2,1)} %param.4) | data formatting | bytes 25165824 | tf_op args[0]
  23.8 0.0 copy-start.1
  23.8 6.5 %all-to-all-start = ((bf16[128,4,12288]{0,2,1:T(8,128)(2,1)}), bf16[128,4,12288]{0,2,1:T(8,128)(2,1)}, u32[]{:S(2)}, u32[]{:S(2)}) async-start(bf16[128,4,12288]{0,2,1:T(8,128)(2,1)} %bitcast.22), calls=%async_computation | async-start | bytes 25165824 | tf_op jit(solution)/shard_map/all_to_all | solution.py:21
  30.4 0.0 copy-done.1
  30.4 0.8 dynamic-slice_sqrt_fusion
  31.2 273.7 %all-to-all-done = bf16[128,4,12288]{0,2,1:T(8,128)(2,1)} async-done(((bf16[128,4,12288]{0,2,1:T(8,128)(2,1)}), bf16[128,4,12288]{0,2,1:T(8,128)(2,1)}, u32[]{:S(2)}, u32[]{:S(2)}) %all-to-all-start) | async-done | bytes 12582944 | tf_op jit(solution)/shard_map/all_to_all | solution.py:21
  304.9 6.8 %convert_reduce_fusion = f32[12288]{0:T(1024)S(1)} fusion(bf16[128,4,12288]{0,2,1:T(8,128)(2,1)} %all-to-all-done), kind=kLoop, calls=%fused_computation.2 | loop fusion | flops 12570624 | bytes 12632064 | tf_op jit(solution)/shard_map/reduce_sum | solution.py:22
  311.7 11.7 %fusion.5 = bf16[4,128,12288]{1,2,0:T(8,128)(2,1)} fusion(bf16[128,4,12288]{0,2,1:T(8,128)(2,1)} %all-to-all-done, f32[12288]{0:T(1024)S(1)} %broadcast_multiply_fusion, f32[12288]{0:T(1024)S(1)} %dynamic-slice_sqrt_fusion), kind=kLoop, calls=%fused_computation.10 | loop fusion | flops 25165824 | bytes 25264128 | tf_op jit(solution)/shard_map/mul | solution.py:25
  323.5 16.7 %copy.9 = bf16[4,128,12288]{2,1,0:T(8,128)(2,1)} copy(bf16[4,128,12288]{1,2,0:T(8,128)(2,1)} %fusion.5) | data formatting | bytes 25165824 | tf_op jit(solution)/shard_map/mul | solution.py:25
  340.2 13.9 %convert_bitcast_fusion = f32[4,128,12288]{1,2,0:T(8,128)} fusion(bf16[128,4,12288]{0,2,1:T(8,128)(2,1)} %all-to-all-done), kind=kLoop, calls=%fused_computation | loop fusion | flops 6291456 | bytes 37748736 | tf_op jit(solution)/shard_map/convert_element_type | solution.py:25
  354.0 24.6 %copy.10 = f32[4,128,12288]{2,1,0:T(8,128)} copy(f32[4,128,12288]{1,2,0:T(8,128)} %convert_bitcast_fusion) | data formatting | bytes 50331648 | tf_op jit(solution)/shard_map/convert_element_type | solution.py:25
  378.7 10.0 %fusion.3 = bf16[512,12288]{1,0:T(8,128)(2,1)S(1)} fusion(f32[4,128,12288]{2,1,0:T(8,128)} %copy.10, f32[12288]{0:T(1024)S(1)} %broadcast_multiply_fusion, f32[12288]{0:T(1024)S(1)} %dynamic-slice_sqrt_fusion), kind=kLoop, calls=%fused_computation.7 | loop fusion | flops 18874368 | bytes 37847040 | tf_op jit(solution)/shard_map/convert_element_type | solution.py:25
  388.7 0.0 copy-done
  388.7 3.5 fusion.4
  392.2 3.6 all-to-all-start.1
  395.8 0.0 reduce-scatter.3.cloned.1.call-start
  395.8 15.6 %fusion.6 = bf16[512,512]{1,0:T(8,128)(2,1)} fusion(bf16[512,12288]{1,0:T(8,128)(2,1)} %bitcast.23), kind=kOutput, calls=%fused_computation.12 | convolution fusion | flops 6442975232 | bytes 13107200 | tf_op jit(solution)/shard_map/dot_general | solution.py:8
  411.4 0.0 reduce-scatter.3.cloned.1.call-update
  411.4 0.0 reduce-scatter.5.cloned.1.call-start
  411.5 26.8 %reduce-scatter.3.cloned.1.call-done = bf16[128,512]{1,0:T(8,128)(2,1)} async-done(((bf16[512,512]{1,0:T(8,128)(2,1)}), bf16[128,512]{1,0:T(8,128)(2,1)}) %reduce-scatter.3.cloned.1.call-update) | async-done | bytes 131088 | tf_op jit(solution)/shard_map/reduce_scatter | solution.py:29
  438.2 0.0 reduce-scatter.5.cloned.1.call-update
  438.3 36.7 %reduce-scatter.5.cloned.1.call-done = bf16[16,512]{1,0:T(8,128)(2,1)} async-done(((bf16[128,512]{1,0:T(8,128)(2,1)}), bf16[16,512]{1,0:T(8,128)(2,1)}) %reduce-scatter.5.cloned.1.call-update) | async-done | bytes 16400 | tf_op jit(solution)/shard_map/reduce_scatter | solution.py:32
  475.0 1.3 convert_element_type.38
  476.3 0.0 all-to-all-done.1
  476.3 1.3 copy.12
  (2 shorter events, 0.0 us)
Async XLA Ops:
  7.2 381.5 %copy-start = (bf16[512,64]{0,1:T(8,128)(2,1)S(1)}, bf16[512,64]{0,1:T(8,128)(2,1)}, u32[]{:S(2)}) copy-start(bf16[512,64]{0,1:T(8,128)(2,1)} %param.6) | copy-start | bytes 196612
  23.8 6.6 %copy-start.1 = (f32[64]{0:T(128)S(1)}, f32[64]{0:T(128)}, u32[]{:S(2)}) copy-start(f32[64]{0:T(128)} %param.7) | copy-start | bytes 772
  23.8 281.1 %all-to-all-start = ((bf16[128,4,12288]{0,2,1:T(8,128)(2,1)}), bf16[128,4,12288]{0,2,1:T(8,128)(2,1)}, u32[]{:S(2)}, u32[]{:S(2)}) async-start(bf16[128,4,12288]{0,2,1:T(8,128)(2,1)} %bitcast.22), calls=%async_computation | async-start | bytes 25165824 | tf_op jit(solution)/shard_map/all_to_all | solution.py:21
  392.2 84.1 %all-to-all-start.1 = ((bf16[4,16,12288]{2,1,0:T(8,128)(2,1)}), bf16[4,16,12288]{2,1,0:T(8,128)(2,1)S(1)}, u32[]{:S(2)}, u32[]{:S(2)}) async-start(bf16[4,16,12288]{2,1,0:T(8,128)(2,1)} %bitcast.6), calls=%async_computation.3 | async-start | bytes 3145728 | tf_op jit(solution)/shard_map/all_to_all | solution.py:36
  395.8 42.5 %reduce-scatter.3.cloned.1.call-start = ((), (), s32[]{:S(2)}) async-start(), calls=%async_computation.4 | async-start | bytes 655360 | tf_op jit(solution)/shard_map/reduce_scatter | solution.py:29
  411.4 63.6 %reduce-scatter.5.cloned.1.call-start = ((), (), s32[]{:S(2)}) async-start(), calls=%async_computation.5 | async-start | bytes 147456 | tf_op jit(solution)/shard_map/reduce_scatter | solution.py:32
Sparse Core Ops, SparseCore 0:
  411.5 26.6 reduce-scatter.2
  441.2 33.6 reduce-scatter.4
where the time goes:
time: 486 us; the launch traced here: 484 us
  waiting for transfers between devices  337 us (69%)
  local copies, waits for them, and re-layouts  60.1 us (12%)
  other arithmetic  43.7 us (9%)
  matrix products  19.1 us (4%)
  between operations  14.1 us (3%)
  starting transfers between devices  10.2 us (2%)
    all_to_all x1, waiting for transfers between devices, local(): lax.all_to_all(snapshots, 'tm', split_axis=1, concat_axis=0, tiled=True)  274 us
    reduce_scatter x1, waiting for transfers between devices, local(): lax.psum_scatter(row_sums, 'space', scatter_dimension=0, tiled=True)  36.7 us
    reduce_scatter x1, waiting for transfers between devices, local(): lax.psum_scatter(partial_gram.astype(jnp.bfloat16), 'tm', scatter_dimensi...  26.8 us
    convert_element_type x1, local copies, waits for them, and re-layouts, local(): columns.astype(jnp.float32) - mean[None, :]  24.6 us
    mul x1, local copies, waits for them, and re-layouts, local(): own_root[None, :] * (columns.astype(jnp.float32) - mean[None, :])  16.7 us
    unnamed x5, local copies, waits for them, and re-layouts  16.7 us
    dot_general x1, matrix products, gram_local(): lax.dot_general(weighted, weighted, (((1,), (1,)), ((), ())), preferred_e...  15.6 us
    convert_element_type x1, other arithmetic, local(): columns.astype(jnp.float32) - mean[None, :]  13.9 us
  transfers between devices with their start and end apart: 4, of which 3 were waited for; matrix products, arithmetic and copies ran while one was open for 4% of the time, Pallas kernels for 0%

commit v1 on v0

--- a/solution.py
+++ b/solution.py
@@ -2,6 +2,7 @@
 import jax.numpy as jnp
 from jax import lax
 from jax.sharding import PartitionSpec as P
+from jax.lax import all_to_all, axis_size
 
 
 def gram_local(weighted):
@@ -18,7 +19,9 @@
     cells = cell_dev * space_count
     sub_cells = cell_dev // tm_count
     tm_index = lax.axis_index("tm")
-    columns = lax.all_to_all(snapshots, "tm", split_axis=1, concat_axis=0, tiled=True)
+    columns = jnp.concatenate(
+        all_to_all(jnp.stack(jnp.split(snapshots, axis_size("tm"), axis=1)), "tm", 0, 0), axis=0
+    )
     mean = jnp.sum(columns.astype(jnp.float32), axis=0) / times
     root = jnp.sqrt(area_weight)
     own_root = lax.dynamic_slice_in_dim(root, tm_index * sub_cells, sub_cells, 0)

time: 486 us -> 410 us (0.84)
  local copies, waits for them, and re-layouts: 60.1 us -> 7.3 us
  other arithmetic: 43.7 us -> 29.4 us
  matrix products: 19.1 us -> 10.9 us
    convert_element_type x1 -> x0, local copies, waits for them, and re-layouts: 24.6 us -> none  [local(): columns.astype(jnp.float32) - mean[None, :]]
    mul x1 -> x0, local copies, waits for them, and re-layouts: 16.7 us -> none  [local(): own_root[None, :] * (columns.astype(jnp.float32) - mean[None, :])]
    unnamed x5 -> x6, local copies, waits for them, and re-layouts: 16.7 us -> 0.02 us
    convert_element_type x1 -> x0, other arithmetic: 13.9 us -> none  [local(): columns.astype(jnp.float32) - mean[None, :]]
    mul x1 -> x0, other arithmetic: 11.7 us -> none  [local(): own_root[None, :] * (columns.astype(jnp.float32) - mean[None, :])]
    dot_general x1, matrix products: 15.6 us -> 7.46 us  [gram_local(): lax.dot_general(weighted, weighted, (((1,), (1,)), ((), ())), preferred_e...]
    another operation x0 -> x1, other arithmetic: none -> 5.5 us  [local(): jnp.stack(jnp.split(snapshots, axis_size('tm'), axis=1))]
    another operation x0 -> x1, local copies, waits for them, and re-layouts: none -> 5.2 us  [local(): jnp.stack(jnp.split(snapshots, axis_size('tm'), axis=1))]
where the time goes in v1:
time: 410 us
  waiting for transfers between devices  337 us (82%)
  other arithmetic  29.4 us (7%)
  between operations  14.1 us (3%)
  matrix products  10.9 us (3%)
  starting transfers between devices  10.3 us (3%)
  local copies, waits for them, and re-layouts  7.3 us (2%)
    all_to_all x1, waiting for transfers between devices, local(): all_to_all(jnp.stack(jnp.split(snapshots, axis_size('tm'), axis=1)), 'tm'...  274 us
    reduce_scatter x1, waiting for transfers between devices, local(): lax.psum_scatter(row_sums, 'space', scatter_dimension=0, tiled=True)  36.4 us
    reduce_scatter x1, waiting for transfers between devices, local(): lax.psum_scatter(partial_gram.astype(jnp.bfloat16), 'tm', scatter_dimensi...  27.2 us
    convert_element_type x2, other arithmetic, local(): (own_root[None, :] * (columns.astype(jnp.float32) - mean[None, :])).astyp...  14.9 us
  transfers between devices with their start and end apart: 4, of which 3 were waited for; matrix products, arithmetic and copies ran while one was open for 4% of the time, Pallas kernels for 0%

profile of v1, /device:TPU:0, one launch (start us, length us, event | category | flops | bytes accessed | tf_op | source)
XLA Modules:
  0.0 409.5 jit_solution(1710001234131609638)
XLA Ops:
  7.2 0.0 copy-start
  7.2 5.2 %slice_bitcast_fusion.3 = (bf16[1,128,12288]{2,1,0:T(8,128)(2,1)S(1)}, bf16[1,128,12288]{2,1,0:T(8,128)(2,1)S(1)}, bf16[1,128,12288]{2,1,0:T(8,128)(2,1)S(1)}, bf16[1,128,12288]{2,1,0:T(8,128)(2,1)S(1)}) fusion(bf16[128,49152]{1,0:T(8,128)(2,1)} %param.4), kind=kLoop, calls=%fused_computation.11 | loop fusion | bytes 25165824 | tf_op jit(solution)/shard_map/stack | solution.py:23
  12.4 5.5 %pad_maximum_fusion = bf16[4,128,12288]{2,1,0:T(8,128)(2,1)} fusion(bf16[1,128,12288]{2,1,0:T(8,128)(2,1)S(1)} %get-tuple-element.4, bf16[1,128,12288]{2,1,0:T(8,128)(2,1)S(1)} %get-tuple-element.5, bf16[1,128,12288]{2,1,0:T(8,128)(2,1)S(1)} %get-tuple-element.3, bf16[1,128,12288]{2,1,0:T(8,128)(2,1)S(1)} %get-tuple-element.2), kind=kLoop, calls=%fused_computation.6 | loop fusion | flops 18874368 | bytes 25165824 | tf_op jit(solution)/shard_map/stack | solution.py:23
  17.9 0.0 copy-start.2
  17.9 6.5 %all-to-all-start = ((bf16[4,128,12288]{2,1,0:T(8,128)(2,1)}), bf16[4,128,12288]{2,1,0:T(8,128)(2,1)}, u32[]{:S(2)}, u32[]{:S(2)}) async-start(bf16[4,128,12288]{2,1,0:T(8,128)(2,1)} %pad_maximum_fusion), calls=%async_computation | async-start | bytes 25165824 | tf_op jit(solution)/shard_map/all_to_all | solution.py:23
  24.4 0.0 copy-done.2
  24.4 0.8 dynamic-slice_sqrt_fusion
  25.2 273.9 %all-to-all-done = bf16[4,128,12288]{2,1,0:T(8,128)(2,1)} async-done(((bf16[4,128,12288]{2,1,0:T(8,128)(2,1)}), bf16[4,128,12288]{2,1,0:T(8,128)(2,1)}, u32[]{:S(2)}, u32[]{:S(2)}) %all-to-all-start) | async-done | bytes 12582944 | tf_op jit(solution)/shard_map/all_to_all | solution.py:23
  299.1 7.7 %convert_reduce_fusion = f32[12288]{0:T(1024)S(1)} fusion(bf16[4,128,12288]{2,1,0:T(8,128)(2,1)} %all-to-all-done), kind=kLoop, calls=%fused_computation.7 | loop fusion | flops 12570624 | bytes 12632064 | tf_op jit(solution)/shard_map/reduce_sum | solution.py:25
  306.8 7.4 %fusion.1 = bf16[512,12288]{1,0:T(8,128)(2,1)S(1)} fusion(f32[12288]{0:T(1024)S(1)} %broadcast_multiply_fusion, f32[12288]{0:T(1024)S(1)} %dynamic-slice_sqrt_fusion, bf16[4,128,12288]{2,1,0:T(8,128)(2,1)} %all-to-all-done), kind=kLoop, calls=%fused_computation.2 | loop fusion | flops 25165824 | bytes 25264128 | tf_op jit(solution)/shard_map/convert_element_type | solution.py:28
  314.3 0.0 copy-done
  314.3 3.5 fusion.2
  317.7 3.6 all-to-all-start.1
  321.3 0.2 reduce-scatter.3.cloned.1.call-start
  321.6 7.4 %multiply_convert_fusion = bf16[4,128,12288]{2,1,0:T(8,128)(2,1)S(1)} fusion(f32[12288]{0:T(1024)S(1)} %broadcast_multiply_fusion, bf16[4,128,12288]{2,1,0:T(8,128)(2,1)} %all-to-all-done, f32[12288]{0:T(1024)S(1)} %dynamic-slice_sqrt_fusion), kind=kLoop, calls=%fused_computation.3 | loop fusion | flops 25165824 | bytes 25264128 | tf_op jit(solution)/shard_map/convert_element_type | solution.py:28
  329.0 0.0 copy-start.1
  329.0 7.5 %fusion.3 = bf16[512,512]{1,0:T(8,128)(2,1)} fusion(bf16[512,12288]{1,0:T(8,128)(2,1)S(1)} %bitcast.25), kind=kOutput, calls=%fused_computation.13 | convolution fusion | flops 6442975232 | bytes 13107200 | tf_op jit(solution)/shard_map/dot_general | solution.py:9
  336.5 0.0 reduce-scatter.3.cloned.1.call-update
  336.5 0.0 reduce-scatter.5.cloned.1.call-start
  336.5 27.2 %reduce-scatter.3.cloned.1.call-done = bf16[128,512]{1,0:T(8,128)(2,1)} async-done(((bf16[512,512]{1,0:T(8,128)(2,1)}), bf16[128,512]{1,0:T(8,128)(2,1)}) %reduce-scatter.3.cloned.1.call-update) | async-done | bytes 131088 | tf_op jit(solution)/shard_map/reduce_scatter | solution.py:32
  363.7 0.0 reduce-scatter.5.cloned.1.call-update
  363.7 36.4 %reduce-scatter.5.cloned.1.call-done = bf16[16,512]{1,0:T(8,128)(2,1)} async-done(((bf16[128,512]{1,0:T(8,128)(2,1)}), bf16[16,512]{1,0:T(8,128)(2,1)}) %reduce-scatter.5.cloned.1.call-update) | async-done | bytes 16400 | tf_op jit(solution)/shard_map/reduce_scatter | solution.py:35
  400.1 1.3 convert_element_type.37
  401.4 0.0 all-to-all-done.1
  401.4 1.3 copy.7
  402.7 0.0 copy-done.1
  (2 shorter events, 0.0 us)
Async XLA Ops:
  7.2 307.1 %copy-start = (bf16[512,64]{0,1:T(8,128)(2,1)S(1)}, bf16[512,64]{0,1:T(8,128)(2,1)}, u32[]{:S(2)}) copy-start(bf16[512,64]{0,1:T(8,128)(2,1)} %param.6) | copy-start | bytes 196612
  17.9 6.5 %copy-start.2 = (f32[64]{0:T(128)S(1)}, f32[64]{0:T(128)}, u32[]{:S(2)}) copy-start(f32[64]{0:T(128)} %param.7) | copy-start | bytes 772
  17.9 281.2 %all-to-all-start = ((bf16[4,128,12288]{2,1,0:T(8,128)(2,1)}), bf16[4,128,12288]{2,1,0:T(8,128)(2,1)}, u32[]{:S(2)}, u32[]{:S(2)}) async-start(bf16[4,128,12288]{2,1,0:T(8,128)(2,1)} %pad_maximum_fusion), calls=%async_computation | async-start | bytes 25165824 | tf_op jit(solution)/shard_map/all_to_all | solution.py:23
  317.7 83.7 %all-to-all-start.1 = ((bf16[4,16,12288]{2,1,0:T(8,128)(2,1)}), bf16[4,16,12288]{2,1,0:T(8,128)(2,1)S(1)}, u32[]{:S(2)}, u32[]{:S(2)}) async-start(bf16[4,16,12288]{2,1,0:T(8,128)(2,1)} %bitcast.27), calls=%async_computation.3 | async-start | bytes 3145728 | tf_op jit(solution)/shard_map/all_to_all | solution.py:39
  321.3 42.4 %reduce-scatter.3.cloned.1.call-start = ((), (), s32[]{:S(2)}) async-start(), calls=%async_computation.4 | async-start | bytes 655360 | tf_op jit(solution)/shard_map/reduce_scatter | solution.py:32
  329.0 73.7 %copy-start.1 = (bf16[512,64]{0,1:T(8,128)(2,1)S(1)}, bf16[512,64]{0,1:T(8,128)(2,1)}, u32[]{:S(2)}) copy-start(bf16[512,64]{0,1:T(8,128)(2,1)} %param.6) | copy-start | bytes 196612
  336.5 63.6 %reduce-scatter.5.cloned.1.call-start = ((), (), s32[]{:S(2)}) async-start(), calls=%async_computation.5 | async-start | bytes 147456 | tf_op jit(solution)/shard_map/reduce_scatter | solution.py:35
Sparse Core Ops, SparseCore 0:
  336.6 27.0 reduce-scatter.2
  366.7 33.3 reduce-scatter.4
